TPU v7x, 32 devices: a whole 2x2x4 slice. The times are simulated.
32 devices in a mesh: row: 8 (over z, y), col: 4 (over x, core).
Axes of the slice: x: 2, y: 2, z: 4, core: 2. Of those that a mesh axis runs over, the one named last changes fastest.
Arguments:
- tokens: bfloat16 [6272, 2048], P('row', 'col'), may hold values from -6 to 6
- first_gain: float32 [1024], P('col'), may hold values from 0.1 to 1.9
- first_shift: float32 [1024], P('col'), may hold values from -1.5 to 1.5
- inward_weight: bfloat16 [1024, 3, 1024], P('row', None, 'col'), may hold values from -0.25 to 0.25
- attention_bias: float32 [2, 1024], P(None, 'col'), may hold values from -2.5 to 2.5
- output_weight: bfloat16 [1024, 1024], P('col', 'row'), may hold values from -2 to 2
- output_bias: float32 [1024], P('col'), may hold values from -2.5 to 2.5
- second_gain: float32 [1024], P('col'), may hold values from 0.1 to 1.9
- second_shift: float32 [1024], P('col'), may hold values from -1.5 to 1.5
- expand_weight: bfloat16 [1024, 4096], P('row', 'col'), may hold values from -0.1875 to 0.1875
- expand_bias: float32 [4096], P('col'), may hold values from -2.5 to 2.5
- reduce_weight: bfloat16 [4096, 1024], P('col', 'row'), may hold values from -0.125 to 0.125
- reduce_bias: float32 [1024], P('col'), may hold values from -2.5 to 2.5
- cotangent: bfloat16 [6272, 2048], P('row', 'col'), may hold values from -6 to 6
Outputs:
- layer_output: bfloat16 [6272, 2048], P('row', 'col')
- tokens_grad: float32 [6272, 2048], P('row', 'col')
- first_gain_grad: float32 [1024], P('col')
- first_shift_grad: float32 [1024], P('col')
- inward_grad: float32 [1024, 3, 1024], P('row', None, 'col')
- attention_bias_grad: float32 [2, 1024], P(None, 'col')
- output_grad: float32 [1024, 1024], P('col', 'row')
- output_bias_grad: float32 [1024], P('col')
- second_gain_grad: float32 [1024], P('col')
- second_shift_grad: float32 [1024], P('col')
- expand_grad: float32 [1024, 4096], P('row', 'col')
- expand_bias_grad: float32 [4096], P('col')
- reduce_grad: float32 [4096, 1024], P('col', 'row')
- reduce_bias_grad: float32 [1024], P('col')
All inputs are finite; a program needn't handle non-finite values.
Results may differ from a plain program's by a relative error of at most 0.015.
The roundings to bfloat16 on the way count: a program that leaves them out, or rounds other values in their place, can miss the bound.
Values may be sent and summed in bfloat16 or wider, within the bound.
A program may use at most 192 MiB of HBM per device.

v0:
```python
import jax
import jax.numpy as jnp
from jax import lax
from jax.sharding import PartitionSpec as P

HEAD_DIM = 64
SEQ = 1568
EPSILON = 1e-06
CONTRACT_ROWS = (((0,), (0,)), ((), ()))
CONTRACT_COLS = (((1,), (1,)), ((), ()))


def norm_forward(values, gain, shift, full_width):
    row_total = lax.psum(jnp.sum(values, axis=1), "col")
    centred = values - (row_total / full_width)[:, None]
    row_square = lax.psum(jnp.sum(centred * centred, axis=1), "col")
    inverse = lax.rsqrt(row_square / full_width + EPSILON)
    unit_rows = centred * inverse[:, None]
    return (unit_rows, inverse, unit_rows * gain + shift)


def norm_backward(incoming, unit_rows, inverse, gain, full_width):
    scaled = incoming * gain
    plain_sum, cross_sum = lax.psum(
        (jnp.sum(scaled, axis=1), jnp.sum(scaled * unit_rows, axis=1)), "col"
    )
    result = inverse[:, None] * (
        scaled - (plain_sum / full_width)[:, None] - unit_rows * (cross_sum / full_width)[:, None]
    )
    return (result, jnp.sum(incoming * unit_rows, axis=0), jnp.sum(incoming, axis=0))


def spread_features(values):
    return lax.all_gather(values, "col", axis=1, tiled=True)


def sum_partials(values):
    return lax.psum_scatter(values, "col", scatter_dimension=1, tiled=True)


def spread_grads(values):
    return lax.all_gather(values, "col", axis=1, tiled=True)


def sum_grad_partials(values):
    return lax.psum_scatter(values, "col", scatter_dimension=1, tiled=True)


def fetch_weights(inward_weight, output_weight, expand_weight, reduce_weight):
    return (
        lax.all_gather(inward_weight, "row", axis=0, tiled=True),
        lax.all_gather(output_weight, "row", axis=1, tiled=True),
        lax.all_gather(expand_weight, "row", axis=0, tiled=True),
        lax.all_gather(reduce_weight, "row", axis=1, tiled=True),
    )


def attend_clip(queries, key_rows, value_rows, score_scale):
    seq_len = queries.shape[0]
    blocks = queries.reshape((2, seq_len // 2) + queries.shape[1:])

    def one_block(query_part):
        scores = (
            jnp.einsum("qhd,khd->hqk", query_part, key_rows, preferred_element_type=jnp.float32)
            * score_scale
        )
        row_peak = jnp.max(scores, axis=-1, keepdims=True)
        exponent = jnp.exp(scores - row_peak)
        row_sum = jnp.sum(exponent, axis=-1, keepdims=True)
        prob_low = (exponent / row_sum).astype(jnp.bfloat16)
        mixed_rows = jnp.einsum(
            "hqk,khd->qhd", prob_low, value_rows, preferred_element_type=jnp.float32
        )
        return (mixed_rows, (row_peak + jnp.log(row_sum))[..., 0])

    mixed_rows, logsum = lax.map(one_block, blocks)
    return (mixed_rows.reshape(queries.shape), logsum)


def attend_clip_back(queries, key_rows, value_rows, logsum, grad_out, score_scale):
    seq_len = queries.shape[0]
    block_shape = (2, seq_len // 2) + queries.shape[1:]

    def step_block(carry, pieces):
        key_acc, value_acc = carry
        query_part, grad_part, log_part = pieces
        scores = (
            jnp.einsum("qhd,khd->hqk", query_part, key_rows, preferred_element_type=jnp.float32)
            * score_scale
        )
        probs = jnp.exp(scores - log_part[..., None])
        grad_probs = jnp.einsum(
            "qhd,khd->hqk", grad_part, value_rows, preferred_element_type=jnp.float32
        )
        inner_sum = jnp.sum(probs * grad_probs, axis=-1, keepdims=True)
        grad_scores = (probs * (grad_probs - inner_sum)).astype(jnp.bfloat16)
        query_grad = (
            jnp.einsum("hqk,khd->qhd", grad_scores, key_rows, preferred_element_type=jnp.float32)
            * score_scale
        )
        key_acc = key_acc + jnp.einsum(
            "hqk,qhd->khd", grad_scores, query_part, preferred_element_type=jnp.float32
        )
        value_acc = value_acc + jnp.einsum(
            "hqk,qhd->khd",
            probs.astype(jnp.bfloat16),
            grad_part,
            preferred_element_type=jnp.float32,
        )
        return ((key_acc, value_acc), query_grad)

    zero_acc = jnp.zeros(key_rows.shape, jnp.float32)
    (key_acc, value_acc), query_grads = lax.scan(
        step_block,
        (zero_acc, zero_acc),
        (queries.reshape(block_shape), grad_out.reshape(block_shape), logsum),
    )
    return (query_grads.reshape(queries.shape), key_acc * score_scale, value_acc)


def forward_pass(
    tokens,
    first_gain,
    first_shift,
    attention_bias,
    output_bias,
    second_gain,
    second_shift,
    expand_bias,
    reduce_bias,
    gathered,
):
    inward_all, output_rows, expand_all, reduce_rows = gathered
    full_width = inward_all.shape[0]
    local_width = inward_all.shape[2]
    row_count = tokens.shape[0]
    clip_shape = (row_count // SEQ, SEQ, local_width // HEAD_DIM, HEAD_DIM)
    score_scale = HEAD_DIM ** (-0.5)
    source = tokens.astype(jnp.float32)
    unit_one, inverse_one, normed_one = norm_forward(source, first_gain, first_shift, full_width)
    normed_all = spread_features(normed_one.astype(jnp.bfloat16))
    projected = jnp.dot(
        normed_all,
        inward_all.reshape(full_width, 3 * local_width),
        preferred_element_type=jnp.float32,
    )
    projected = projected.reshape(row_count, 3, local_width)
    queries = (projected[:, 0] + attention_bias[0]).astype(jnp.bfloat16)
    key_rows = projected[:, 1].astype(jnp.bfloat16)
    value_rows = (projected[:, 2] + attention_bias[1]).astype(jnp.bfloat16)
    mixed_rows, logsum = lax.map(
        lambda clip_parts: attend_clip(clip_parts[0], clip_parts[1], clip_parts[2], score_scale),
        (queries.reshape(clip_shape), key_rows.reshape(clip_shape), value_rows.reshape(clip_shape)),
    )
    mixed_low = mixed_rows.reshape(row_count, local_width).astype(jnp.bfloat16)
    hidden_state = (
        source
        + sum_partials(jnp.dot(mixed_low, output_rows, preferred_element_type=jnp.float32))
        + output_bias
    )
    unit_two, inverse_two, normed_two = norm_forward(
        hidden_state, second_gain, second_shift, full_width
    )
    normed_all_two = spread_features(normed_two.astype(jnp.bfloat16))
    expanded = jnp.dot(normed_all_two, expand_all, preferred_element_type=jnp.float32) + expand_bias
    activated = jax.nn.gelu(expanded, approximate=False).astype(jnp.bfloat16)
    output_value = (
        hidden_state
        + sum_partials(jnp.dot(activated, reduce_rows, preferred_element_type=jnp.float32))
        + reduce_bias
    )
    saved_state = (
        unit_one,
        inverse_one,
        normed_all,
        queries,
        key_rows,
        value_rows,
        logsum,
        mixed_low,
        unit_two,
        inverse_two,
        normed_all_two,
        expanded,
        activated,
    )
    return (output_value, saved_state)


def per_device(
    tokens,
    first_gain,
    first_shift,
    inward_weight,
    attention_bias,
    output_weight,
    output_bias,
    second_gain,
    second_shift,
    expand_weight,
    expand_bias,
    reduce_weight,
    reduce_bias,
    cotangent,
):
    packed_width = tokens.shape[1]
    tokens = tokens.reshape(-1, packed_width // 2)
    cotangent = cotangent.reshape(-1, packed_width // 2)
    gathered = fetch_weights(inward_weight, output_weight, expand_weight, reduce_weight)
    output_value, saved_state = forward_pass(
        tokens,
        first_gain,
        first_shift,
        attention_bias,
        output_bias,
        second_gain,
        second_shift,
        expand_bias,
        reduce_bias,
        gathered,
    )
    gathered = fetch_weights(inward_weight, output_weight, expand_weight, reduce_weight)
    unused_value, saved_state = forward_pass(
        tokens,
        first_gain,
        first_shift,
        attention_bias,
        output_bias,
        second_gain,
        second_shift,
        expand_bias,
        reduce_bias,
        gathered,
    )
    inward_all, output_rows, expand_all, reduce_rows = gathered
    (
        unit_one,
        inverse_one,
        normed_all,
        queries,
        key_rows,
        value_rows,
        logsum,
        mixed_low,
        unit_two,
        inverse_two,
        normed_all_two,
        expanded,
        activated,
    ) = saved_state
    full_width = inward_all.shape[0]
    local_width = inward_all.shape[2]
    row_count = tokens.shape[0]
    clip_shape = (row_count // SEQ, SEQ, local_width // HEAD_DIM, HEAD_DIM)
    score_scale = HEAD_DIM ** (-0.5)
    grad_rows = cotangent.astype(jnp.float32)
    grad_all = spread_grads(cotangent)
    grad_act = lax.dot_general(
        grad_all, reduce_rows, CONTRACT_COLS, preferred_element_type=jnp.float32
    )
    reduce_grad = lax.dot_general(
        activated, grad_all, CONTRACT_ROWS, preferred_element_type=jnp.float32
    )
    reduce_bias_grad = jnp.sum(grad_rows, axis=0)
    gelu_value, gelu_back = jax.vjp(
        lambda inner_value: jax.nn.gelu(inner_value, approximate=False), expanded
    )
    grad_expanded = gelu_back(grad_act)[0].astype(jnp.bfloat16)
    expand_grad = lax.dot_general(
        normed_all_two, grad_expanded, CONTRACT_ROWS, preferred_element_type=jnp.float32
    )
    expand_bias_grad = jnp.sum(grad_expanded.astype(jnp.float32), axis=0)
    grad_normed_two = sum_grad_partials(
        lax.dot_general(
            grad_expanded, expand_all, CONTRACT_COLS, preferred_element_type=jnp.float32
        )
    )
    back_two, second_gain_grad, second_shift_grad = norm_backward(
        grad_normed_two, unit_two, inverse_two, second_gain, full_width
    )
    grad_hidden = grad_rows + back_two
    grad_hidden_low = grad_hidden.astype(jnp.bfloat16)
    grad_hidden_all = spread_grads(grad_hidden_low)
    output_grad = lax.dot_general(
        mixed_low, grad_hidden_all, CONTRACT_ROWS, preferred_element_type=jnp.float32
    )
    output_bias_grad = jnp.sum(grad_hidden_low.astype(jnp.float32), axis=0)
    grad_mixed = lax.dot_general(
        grad_hidden_all, output_rows, CONTRACT_COLS, preferred_element_type=jnp.float32
    ).astype(jnp.bfloat16)
    query_grads, key_grads, value_grads = lax.map(
        lambda clip_parts: attend_clip_back(
            clip_parts[0], clip_parts[1], clip_parts[2], clip_parts[3], clip_parts[4], score_scale
        ),
        (
            queries.reshape(clip_shape),
            key_rows.reshape(clip_shape),
            value_rows.reshape(clip_shape),
            logsum,
            grad_mixed.reshape(clip_shape),
        ),
    )
    stacked = jnp.stack(
        [
            query_grads.reshape(row_count, local_width),
            key_grads.reshape(row_count, local_width),
            value_grads.reshape(row_count, local_width),
        ],
        axis=1,
    ).astype(jnp.bfloat16)
    attention_bias_grad = jnp.stack(
        [
            jnp.sum(stacked[:, 0].astype(jnp.float32), axis=0),
            jnp.sum(stacked[:, 2].astype(jnp.float32), axis=0),
        ]
    )
    flat_grads = stacked.reshape(row_count, 3 * local_width)
    inward_grad = lax.dot_general(
        normed_all, flat_grads, CONTRACT_ROWS, preferred_element_type=jnp.float32
    ).reshape(full_width, 3, local_width)
    grad_normed_one = sum_grad_partials(
        lax.dot_general(
            flat_grads,
            inward_all.reshape(full_width, 3 * local_width),
            CONTRACT_COLS,
            preferred_element_type=jnp.float32,
        )
    )
    back_one, first_gain_grad, first_shift_grad = norm_backward(
        grad_normed_one, unit_one, inverse_one, first_gain, full_width
    )
    tokens_grad = grad_hidden + back_one
    inward_grad, output_grad, expand_grad, reduce_grad = (
        lax.psum_scatter(
            inward_grad.astype(jnp.bfloat16), "row", scatter_dimension=0, tiled=True
        ).astype(jnp.float32),
        lax.psum_scatter(
            output_grad.astype(jnp.bfloat16), "row", scatter_dimension=1, tiled=True
        ).astype(jnp.float32),
        lax.psum_scatter(
            expand_grad.astype(jnp.bfloat16), "row", scatter_dimension=0, tiled=True
        ).astype(jnp.float32),
        lax.psum_scatter(
            reduce_grad.astype(jnp.bfloat16), "row", scatter_dimension=1, tiled=True
        ).astype(jnp.float32),
    )
    (
        first_gain_grad,
        first_shift_grad,
        attention_bias_grad,
        output_bias_grad,
        second_gain_grad,
        second_shift_grad,
        expand_bias_grad,
        reduce_bias_grad,
    ) = lax.psum(
        (
            first_gain_grad,
            first_shift_grad,
            attention_bias_grad,
            output_bias_grad,
            second_gain_grad,
            second_shift_grad,
            expand_bias_grad,
            reduce_bias_grad,
        ),
        "row",
    )
    return (
        output_value.astype(jnp.bfloat16).reshape(-1, packed_width),
        tokens_grad.reshape(-1, packed_width),
        first_gain_grad,
        first_shift_grad,
        inward_grad,
        attention_bias_grad,
        output_grad,
        output_bias_grad,
        second_gain_grad,
        second_shift_grad,
        expand_grad,
        expand_bias_grad,
        reduce_grad,
        reduce_bias_grad,
    )


def solution(mesh):
    in_specs = (
        P("row", "col"),
        P("col"),
        P("col"),
        P("row", None, "col"),
        P(None, "col"),
        P("col", "row"),
        P("col"),
        P("col"),
        P("col"),
        P("row", "col"),
        P("col"),
        P("col", "row"),
        P("col"),
        P("row", "col"),
    )
    out_specs = (
        P("row", "col"),
        P("row", "col"),
        P("col"),
        P("col"),
        P("row", None, "col"),
        P(None, "col"),
        P("col", "row"),
        P("col"),
        P("col"),
        P("col"),
        P("row", "col"),
        P("col"),
        P("col", "row"),
        P("col"),
    )
    return jax.shard_map(
        per_device, mesh=mesh, in_specs=in_specs, out_specs=out_specs, check_vma=False
    )
```

profile of v0, /device:TPU:0, one launch (start us, length us, event | category | flops | bytes accessed | tf_op | source)
XLA Modules:
  0.0 1172.3 jit_solution(17945256681787545454)
XLA Ops:
  27.5 32.0 %all_gather.34 = bf16[256,1024]{1,0:T(8,128)(2,1)} all-gather(bf16[256,128]{1,0:T(8,128)(2,1)S(1)} %copy-done.18), channel_id=1, replica_groups=mesh['row'=8,'col'=4] {'row'}, dimensions={1}, use_global_device_ids=true | all-gather | bytes 589824 | tf_op jit(solution)/shard_map/all_gather | solution.py:52
  63.6 29.1 %all-gather.9.cloned.1.call-done = bf16[1568,1024]{1,0:T(8,128)(2,1)} async-done(((bf16[1568,256]{1,0:T(8,128)(2,1)}), bf16[1568,1024]{1,0:T(8,128)(2,1)}) %all-gather.9.cloned.1.call-update) | async-done | bytes 3211280 | tf_op jit(solution)/shard_map/all_gather | solution.py:34
  109.3 34.0 %while.64 = (s32[]{:T(128)}, bf16[2,784,4,64]{1,3,2,0:T(8,128)(2,1)S(1)}, bf16[2,784,4,64]{1,3,2,0:T(8,128)(2,1)}, bf16[1568,4,64]{0,2,1:T(8,128)(2,1)}, bf16[1568,4,64]{0,2,1:T(8,128)(2,1)}, /*index=5*/s32[]{:T(128)}) while((s32[]{:T(128)}, bf16[2,784,4,64]{1,3,2,0:T(8,128)(2,1)S(1)}, bf16[2,784,4,64]{1,3,2,0:T(8,128)(2,1)}, ...), condition=%wide.region_7.0_spmd, body=%wide.region_4.7_spmd.sunk | while | flops 1922650112 | bytes 4304209 | solution.py:76
  117.2 9.0 fusion.208
  149.7 30.1 %while.65 = (s32[]{:T(128)}, bf16[2,784,4,64]{1,3,2,0:T(8,128)(2,1)}, f32[2,4,784]{2,1,0:T(4,128)S(1)}, bf16[2,784,4,64]{1,3,2,0:T(8,128)(2,1)}, bf16[1568,4,64]...) while((s32[]{:T(128)}, bf16[2,784,4,64]{1,3,2,0:T(8,128)(2,1)}, ...), condition=%wide.region_17.18_spmd, body=%wide.region_14.17_spmd.sunk | while | flops 1303067648 | bytes 62078304 | solution.py:76
  188.3 19.6 %reduce-scatter.14.cloned.1.call-done = f32[1568,256]{1,0:T(8,128)} async-done(((f32[1568,1024]{1,0:T(8,128)}), f32[1568,256]{1,0:T(8,128)}) %reduce-scatter.14.cloned.1.call-update) | async-done | bytes 1605648 | tf_op jit(solution)/shard_map/reduce_scatter | solution.py:38
  207.9 61.8 %reduce-scatter.18.cloned.1.call-done = f32[1568,256]{1,0:T(8,128)} async-done(((f32[1568,1024]{1,0:T(8,128)}), f32[1568,256]{1,0:T(8,128)}) %reduce-scatter.18.cloned.1.call-update) | async-done | bytes 1605648 | tf_op jit(solution)/shard_map/reduce_scatter | solution.py:38
  290.8 30.3 %all-gather.15.cloned.1.call-done = bf16[1024,1024]{1,0:T(8,128)(2,1)} async-done(((bf16[128,1024]{1,0:T(8,128)(2,1)}), bf16[1024,1024]{1,0:T(8,128)(2,1)}) %all-gather.15.cloned.1.call-update) | async-done | bytes 2097168 | tf_op jit(solution)/shard_map/all_gather | solution.py:53
  321.1 29.8 %all-gather.19.cloned.1.call-done = bf16[1568,1024]{1,0:T(8,128)(2,1)} async-done(((bf16[1568,256]{1,0:T(8,128)(2,1)}), bf16[1568,1024]{1,0:T(8,128)(2,1)}) %all-gather.19.cloned.1.call-update) | async-done | bytes 3211280 | tf_op jit(solution)/shard_map/all_gather | solution.py:34
  359.6 44.5 %all-gather.17.cloned.1.call-done = bf16[1024,1024]{1,0:T(8,128)(2,1)} async-done(((bf16[1024,128]{1,0:T(8,128)(2,1)}), bf16[1024,1024]{1,0:T(8,128)(2,1)}) %all-gather.17.cloned.1.call-update) | async-done | bytes 2097168 | tf_op jit(solution)/shard_map/all_gather | solution.py:54
  404.1 29.1 %all-gather.21.cloned.1.call-done = bf16[1568,1024]{1,0:T(8,128)(2,1)} async-done(((bf16[1568,256]{1,0:T(8,128)(2,1)}), bf16[1568,1024]{1,0:T(8,128)(2,1)}) %all-gather.21.cloned.1.call-update) | async-done | bytes 3211280 | tf_op jit(solution)/shard_map/all_gather | solution.py:42
  433.1 22.4 %convert_reduce_fusion = (f32[1024]{0:T(1024)}, bf16[1568,1024]{1,0:T(8,128)(2,1)S(1)}, f32[1568,1024]{1,0:T(8,128)}) fusion(f32[1568,1024]{1,0:T(8,128)} %fusion.142, f32[1024]{0:T(1024)S(1)} %copy-done.34, bf16[1568,1024]{1,0:T(8,128)(2,1)} %all-gather.21.cloned.1.call-done, bf16[1024,1024]{1,0:T(8,128)(2,1)} %all-gather.17.cloned.1.call-done), kind=kOutput, calls=%fused_computation.69 | convolution fusion | flops 3408755712 | bytes 21372928 | tf_op jit(solution)/shard_map/dot_general | solution.py:258
  463.0 59.1 %reduce-scatter.20.cloned.1.call-done = f32[1568,256]{1,0:T(8,128)} async-done(((f32[1568,1024]{1,0:T(8,128)}), f32[1568,256]{1,0:T(8,128)}) %reduce-scatter.20.cloned.1.call-update) | async-done | bytes 1605648 | tf_op jit(solution)/shard_map/reduce_scatter | solution.py:46
  525.1 10.3 all-reduce.2
  539.3 31.0 %all-gather.23.cloned.1.call-done = bf16[1568,1024]{1,0:T(8,128)(2,1)} async-done(((bf16[1568,256]{1,0:T(8,128)(2,1)}), bf16[1568,1024]{1,0:T(8,128)(2,1)}) %all-gather.23.cloned.1.call-update) | async-done | bytes 3211280 | tf_op jit(solution)/shard_map/all_gather | solution.py:42
  578.0 129.4 %while.66 = (s32[]{:T(128)}, f32[1568,4,64]{0,2,1:T(8,128)}, f32[1568,4,64]{0,2,1:T(8,128)}, bf16[2,784,4,64]{1,3,2,0:T(8,128)(2,1)}, bf16[2,784,4,64]{1,3,2,0:T...) while((s32[]{:T(128)}, f32[1568,4,64]{0,2,1:T(8,128)}, ...), condition=%wide.region_30.31_spmd.clone, body=%wide.region_28.30_spmd.clone.sunk | while | flops 3188179968 | bytes 291960320 | solution.py:113
  578.0 11.2 fusion.222
  589.1 13.9 %multiply_reduce_fusion.15 = (f32[4,784]{1,0:T(4,128)S(1)}, f32[4,784,1568]{2,1,0:T(8,128)}) fusion(f32[4,784,1568]{2,1,0:T(8,128)} %fusion.222, f32[4,784]{1,0:T(4,128)S(1)} %dynamic-slice_bitcast_fusion.2, bf16[1568,4,64]{0,2,1:T(8,128)(2,1)} %get-tuple-element.563, bf16[2,784,4,64]{1,3,2,0:T(8,128)(2,1)} %get-tuple-element.562, s32[]{:T(128)S(6)} %copy.105), kind=kOutput, calls=%fused_computation.37.clone.1 | convolution fusion | flops 649073600 | bytes 41878020 | tf_op jit(solution)/shard_map/while/body/eval_jaxpr/while/body/eval_jaxpr/qhd,khd->hqk/dot_general | solution.py:88
  603.0 18.2 %multiply_convert_fusion.6 = bf16[4,784,1568]{2,1,0:T(8,128)(2,1)} fusion(f32[4,784,1568]{2,1,0:T(8,128)} %get-tuple-element.495, f32[4,784,1568]{2,1,0:T(8,128)} %fusion.222, f32[4,784]{1,0:T(4,128)S(1)} %get-tuple-element.496), kind=kLoop, calls=%fused_computation.36.clone.1 | loop fusion | flops 14751744 | bytes 49185024 | tf_op jit(solution)/shard_map/while/body/eval_jaxpr/while/body/eval_jaxpr/convert_element_type | solution.py:96
  642.4 11.1 fusion.222
  653.5 13.9 %multiply_reduce_fusion.15 = (f32[4,784]{1,0:T(4,128)S(1)}, f32[4,784,1568]{2,1,0:T(8,128)}) fusion(f32[4,784,1568]{2,1,0:T(8,128)} %fusion.222, f32[4,784]{1,0:T(4,128)S(1)} %dynamic-slice_bitcast_fusion.2, bf16[1568,4,64]{0,2,1:T(8,128)(2,1)} %get-tuple-element.563, bf16[2,784,4,64]{1,3,2,0:T(8,128)(2,1)} %get-tuple-element.562, s32[]{:T(128)S(6)} %copy.105), kind=kOutput, calls=%fused_computation.37.clone.1 | convolution fusion | flops 649073600 | bytes 41878020 | tf_op jit(solution)/shard_map/while/body/eval_jaxpr/while/body/eval_jaxpr/qhd,khd->hqk/dot_general | solution.py:88
  667.4 18.2 %multiply_convert_fusion.6 = bf16[4,784,1568]{2,1,0:T(8,128)(2,1)} fusion(f32[4,784,1568]{2,1,0:T(8,128)} %get-tuple-element.495, f32[4,784,1568]{2,1,0:T(8,128)} %fusion.222, f32[4,784]{1,0:T(4,128)S(1)} %get-tuple-element.496), kind=kLoop, calls=%fused_computation.36.clone.1 | loop fusion | flops 14751744 | bytes 49185024 | tf_op jit(solution)/shard_map/while/body/eval_jaxpr/while/body/eval_jaxpr/convert_element_type | solution.py:96
  726.0 57.5 %reduce-scatter.22.cloned.1.call-done = f32[1568,256]{1,0:T(8,128)} async-done(((f32[1568,1024]{1,0:T(8,128)}), f32[1568,256]{1,0:T(8,128)}) %reduce-scatter.22.cloned.1.call-update) | async-done | bytes 1605648 | tf_op jit(solution)/shard_map/reduce_scatter | solution.py:46
  785.9 10.3 all-reduce.1
  797.6 11.4 fusion.95
  835.3 23.6 %fusion.94 = f32[1568,1024]{1,0:T(8,128)} fusion(bf16[1024,1024]{1,0:T(8,128)(2,1)} %all-gather.17.cloned.1.call-done, bf16[1568,1024]{1,0:T(8,128)(2,1)} %all-gather.13.cloned.1.call-done, bf16[1024,1024]{1,0:T(8,128)(2,1)} %all-gather.15.cloned.1.call-done, f32[1024]{0:T(1024)S(1)} %copy-done.35), kind=kOutput, calls=%fused_computation.110 | convolution fusion | flops 6682640384 | bytes 13832192 | tf_op jit(solution)/shard_map/dot_general | solution.py:169
  858.9 40.4 %reduce-scatter.30.cloned.1.call-done = bf16[128,1024]{1,0:T(8,128)(2,1)} async-done(((bf16[1024,1024]{1,0:T(8,128)(2,1)}), bf16[128,1024]{1,0:T(8,128)(2,1)}) %reduce-scatter.30.cloned.1.call-update) | async-done | bytes 262160
  901.3 68.0 %reduce-scatter.26.cloned.1.call-done = bf16[128,1024]{1,0:T(8,128)(2,1)} async-done(((bf16[1024,1024]{1,0:T(8,128)(2,1)}), bf16[128,1024]{1,0:T(8,128)(2,1)}) %reduce-scatter.26.cloned.1.call-update) | async-done | bytes 262160 | tf_op jit(solution)/shard_map/reduce_scatter | solution.py:340
  972.8 60.7 %reduce-scatter.28.cloned.1.call-done = bf16[128,256]{1,0:T(8,128)(2,1)} async-done(((bf16[1024,256]{1,0:T(8,128)(2,1)}), bf16[128,256]{1,0:T(8,128)(2,1)}) %reduce-scatter.28.cloned.1.call-update) | async-done | bytes 65552
  1035.1 67.1 %reduce-scatter.24.cloned.1.call-done = bf16[128,3,256]{2,0,1:T(8,128)(2,1)} async-done(((bf16[1024,3,256]{2,0,1:T(8,128)(2,1)}), bf16[128,3,256]{2,0,1:T(8,128)(2,1)}) %reduce-scatter.24.cloned.1.call-update) | async-done | bytes 196624 | tf_op jit(solution)/shard_map/reduce_scatter | solution.py:334
  1110.1 35.1 %all-reduce = (f32[256]{0:T(256)}, f32[256]{0:T(256)}, f32[2,256]{1,0:T(2,128)}, f32[256]{0:T(256)}, f32[256]{0:T(256)}, /*index=5*/f32[256]{0:T(256)}, f32[1024]{0:T(1024)}, f32[256]{0:T(256)}) all-reduce(f32[256]{0:T(256)S(1)} %get-tuple-element.281, f32[256]{0:T(256)S(1)} %get-tuple-element.288, ...), channel_id=1, replica_groups=mesh['row'=8,'col'=4] {'row'}, use_global_device_ids=true, to_apply=%region_37.38 | all-reduce | flops 3072 | bytes 24576 | tf_op jit(solution)/shard_map/psum | solution.py:356
  1145.2 17.6 %reduce-scatter.16.cloned.1.call-done = f32[1568,256]{1,0:T(8,128)} async-done(((f32[1568,1024]{1,0:T(8,128)}), f32[1568,256]{1,0:T(8,128)}) %reduce-scatter.16.cloned.1.call-update) | async-done | bytes 1605648 | tf_op jit(solution)/shard_map/reduce_scatter | solution.py:38
  (218 shorter events, 270.9 us)
Async XLA Ops:
  7.2 54.7 %all-gather.11.cloned.1.call-start = ((), (), s32[]{:S(2)}) async-start(), calls=%async_computation.10 | async-start | bytes 1769472 | tf_op jit(solution)/shard_map/all_gather | solution.py:51
  7.9 84.8 %all-gather.9.cloned.1.call-start = ((), (), s32[]{:S(2)}) async-start(), calls=%async_computation.9 | async-start | bytes 4014080 | tf_op jit(solution)/shard_map/all_gather | solution.py:34
  9.3 88.1 %copy-start.2 = (f32[1568,256]{1,0:T(8,128)}, f32[1568,256]{1,0:T(8,128)S(1)}, u32[]{:S(2)}) copy-start(f32[1568,256]{1,0:T(8,128)S(1)} %reshape.165) | copy-start | bytes 4816900
  27.2 180.7 %reduce-scatter.14.cloned.1.call-start = ((), (), s32[]{:S(2)}) async-start(), calls=%async_computation.11 | async-start | bytes 8028160 | tf_op jit(solution)/shard_map/reduce_scatter | solution.py:38
  148.6 121.2 %reduce-scatter.18.cloned.1.call-start = ((), (), s32[]{:S(2)}) async-start(), calls=%async_computation.16 | async-start | bytes 8028160 | tf_op jit(solution)/shard_map/reduce_scatter | solution.py:38
  182.5 87.3 %copy-start.3 = (f32[1568,256]{1,0:T(8,128)S(1)}, f32[1568,256]{1,0:T(8,128)}, u32[]{:S(2)}) copy-start(f32[1568,256]{1,0:T(8,128)} %copy-done.2) | copy-start | bytes 4816900
  182.5 87.3 %copy-start.31 = (f32[256]{0:T(256)S(1)}, f32[256]{0:T(256)}, u32[]{:S(2)}) copy-start(f32[256]{0:T(256)} %param.26) | copy-start | bytes 3076
  187.7 98.7 %copy-start.19 = (f32[256]{0:T(256)S(1)}, f32[256]{0:T(256)}, u32[]{:S(2)}) copy-start(f32[256]{0:T(256)} %param.27) | copy-start | bytes 3076
  187.7 98.7 %copy-start.23 = (f32[256]{0:T(256)S(1)}, f32[256]{0:T(256)}, u32[]{:S(2)}) copy-start(f32[256]{0:T(256)} %param.28) | copy-start | bytes 3076
  187.7 133.4 %all-gather.15.cloned.1.call-start = ((), (), s32[]{:S(2)}) async-start(), calls=%async_computation.13 | async-start | bytes 2359296 | tf_op jit(solution)/shard_map/all_gather | solution.py:53
  188.3 162.6 %all-gather.19.cloned.1.call-start = ((), (), s32[]{:S(2)}) async-start(), calls=%async_computation.17 | async-start | bytes 4014080 | tf_op jit(solution)/shard_map/all_gather | solution.py:34
  287.8 116.3 %all-gather.17.cloned.1.call-start = ((), (), s32[]{:S(2)}) async-start(), calls=%async_computation.14 | async-start | bytes 2359296 | tf_op jit(solution)/shard_map/all_gather | solution.py:54
  288.5 144.6 %all-gather.21.cloned.1.call-start = ((), (), s32[]{:S(2)}) async-start(), calls=%async_computation.18 | async-start | bytes 4014080 | tf_op jit(solution)/shard_map/all_gather | solution.py:42
  290.7 142.4 %copy-start.34 = (f32[1024]{0:T(1024)S(1)}, f32[1024]{0:T(1024)}, u32[]{:S(2)}) copy-start(f32[1024]{0:T(1024)} %param.30) | copy-start | bytes 12292
  290.7 231.4 %reduce-scatter.20.cloned.1.call-start = ((), (), s32[]{:S(2)}) async-start(), calls=%async_computation.19 | async-start | bytes 8028160 | tf_op jit(solution)/shard_map/reduce_scatter | solution.py:46
  462.7 72.6 %copy-start.9 = (bf16[1568,256]{1,0:T(8,128)(2,1)S(1)}, bf16[1568,256]{1,0:T(8,128)(2,1)}, u32[]{:S(2)}) copy-start(bf16[1568,256]{1,0:T(8,128)(2,1)} %reshape.162) | copy-start | bytes 2408452
  462.7 107.6 %copy-start.13 = (bf16[256,1024]{1,0:T(8,128)(2,1)S(1)}, bf16[256,1024]{1,0:T(8,128)(2,1)}, u32[]{:S(2)}) copy-start(bf16[256,1024]{1,0:T(8,128)(2,1)} %all_gather.34) | copy-start | bytes 1572868
  462.7 107.6 %all-gather.23.cloned.1.call-start = ((), (), s32[]{:S(2)}) async-start(), calls=%async_computation.20 | async-start | bytes 4014080 | tf_op jit(solution)/shard_map/all_gather | solution.py:42
  539.2 244.2 %reduce-scatter.22.cloned.1.call-start = ((), (), s32[]{:S(2)}) async-start(), calls=%async_computation.21 | async-start | bytes 8028160 | tf_op jit(solution)/shard_map/reduce_scatter | solution.py:46
  724.1 73.6 %copy-start.35 = (f32[1024]{0:T(1024)S(1)}, f32[1024]{0:T(1024)}, u32[]{:S(2)}) copy-start(f32[1024]{0:T(1024)} %param.30) | copy-start | bytes 12292
  724.1 111.2 %all-gather.13.cloned.1.call-start = ((), (), s32[]{:S(2)}) async-start(), calls=%async_computation.12 | async-start | bytes 4014080 | tf_op jit(solution)/shard_map/all_gather | solution.py:34
  797.6 101.7 %reduce-scatter.30.cloned.1.call-start = ((), (), s32[]{:S(2)}) async-start(), calls=%async_computation.25 | async-start | bytes 2359296
  813.1 156.3 %reduce-scatter.26.cloned.1.call-start = ((), (), s32[]{:S(2)}) async-start(), calls=%async_computation.23 | async-start | bytes 2359296 | tf_op jit(solution)/shard_map/reduce_scatter | solution.py:340
  821.9 211.6 %reduce-scatter.28.cloned.1.call-start = ((), (), s32[]{:S(2)}) async-start(), calls=%async_computation.24 | async-start | bytes 589824
  828.1 274.1 %reduce-scatter.24.cloned.1.call-start = ((), (), s32[]{:S(2)}) async-start(), calls=%async_computation.22 | async-start | bytes 1769472 | tf_op jit(solution)/shard_map/reduce_scatter | solution.py:334
  835.1 327.7 %reduce-scatter.16.cloned.1.call-start = ((), (), s32[]{:S(2)}) async-start(), calls=%async_computation.15 | async-start | bytes 8028160 | tf_op jit(solution)/shard_map/reduce_scatter | solution.py:38
  901.3 208.8 %copy-start.25 = (f32[256]{0:T(256)S(1)}, f32[256]{0:T(256)}, u32[]{:S(2)}) copy-start(f32[256]{0:T(256)} %get-tuple-element.279) | copy-start | bytes 3076
  901.3 208.8 %copy-start.26 = (f32[256]{0:T(256)S(1)}, f32[256]{0:T(256)}, u32[]{:S(2)}) copy-start(f32[256]{0:T(256)} %get-tuple-element.287) | copy-start | bytes 3076
  901.3 208.8 %copy-start.27 = (f32[256]{0:T(256)S(1)}, f32[256]{0:T(256)}, u32[]{:S(2)}) copy-start(f32[256]{0:T(256)} %get-tuple-element.348) | copy-start | bytes 3076
  901.3 208.8 %copy-start.28 = (f32[256]{0:T(256)S(1)}, f32[256]{0:T(256)}, u32[]{:S(2)}) copy-start(f32[256]{0:T(256)} %get-tuple-element.363) | copy-start | bytes 3076
  901.3 208.8 %copy-start.29 = (f32[1024]{0:T(1024)S(1)}, f32[1024]{0:T(1024)}, u32[]{:S(2)}) copy-start(f32[1024]{0:T(1024)} %get-tuple-element.345) | copy-start | bytes 12292
  901.3 261.5 %copy-start.32 = (f32[256]{0:T(256)S(1)}, f32[256]{0:T(256)}, u32[]{:S(2)}) copy-start(f32[256]{0:T(256)} %param.32) | copy-start | bytes 3076
  (26 other events, 622.5 us)
Sparse Core Ops, SparseCore 0:
  10.2 51.6 all-gather.10
  64.0 28.6 all-gather.8
  148.7 59.2 reduce-scatter.13
  210.5 59.2 reduce-scatter.17
  271.8 49.2 all-gather.14
  323.1 27.7 all-gather.18
  352.9 51.0 all-gather.16
  405.6 27.4 all-gather.20
  462.9 59.2 reduce-scatter.19
  539.4 30.9 all-gather.22
  724.2 59.2 reduce-scatter.21
  797.7 30.3 all-gather.12
  831.6 67.6 reduce-scatter.29
  902.7 66.6 reduce-scatter.25
  972.5 60.8 reduce-scatter.27
  1037.7 64.4 reduce-scatter.23
  1104.6 58.1 reduce-scatter.15
where the time goes:
time: 1180 us; the launch traced here: 1170 us
  waiting for transfers between devices  650 us (55%)
  matrix products  250 us (21%)
  blocking collectives  114 us (10%)
  other arithmetic  79.1 us (7%)
  local copies, waits for them, and re-layouts  61.6 us (5%)
  between operations  14.8 us (1%)
    reduce_scatter x2, waiting for transfers between devices, sum_grad_partials(): return lax.psum_scatter(values, 'col', scatter_dimension=1, tiled=True)  117 us
    unnamed x19, waiting for transfers between devices  103 us
    reduce_scatter x3, waiting for transfers between devices, sum_partials(): return lax.psum_scatter(values, 'col', scatter_dimension=1, tiled=True)  99 us
    reduce_scatter x1, waiting for transfers between devices, per_device(): lax.psum_scatter(expand_grad.astype(jnp.bfloat16), 'row', scatter_dimensi...  68 us
    reduce_scatter x1, waiting for transfers between devices, per_device(): lax.psum_scatter(inward_grad.astype(jnp.bfloat16), 'row', scatter_dimensi...  67.1 us
    all_gather x2, waiting for transfers between devices, spread_grads(): return lax.all_gather(values, 'col', axis=1, tiled=True)  60.1 us
    all_gather x3, waiting for transfers between devices, spread_features(): return lax.all_gather(values, 'col', axis=1, tiled=True)  58.9 us
    all_gather x1, waiting for transfers between devices, fetch_weights(): lax.all_gather(reduce_weight, 'row', axis=1, tiled=True)  44.5 us
  transfers between devices with their start and end apart: 17, of which 16 were waited for; matrix products, arithmetic and copies ran while one was open for 12% of the time, Pallas kernels for 0%

commit v1 on v0

--- a/solution.py
+++ b/solution.py
@@ -11,7 +11,7 @@
 
 
 def norm_forward(values, gain, shift, full_width):
-    row_total = lax.psum(jnp.sum(values, axis=1), "col")
+    row_total = jnp.sum(lax.all_gather(jnp.sum(values, axis=1), "col"), axis=0)
     centred = values - (row_total / full_width)[:, None]
     row_square = lax.psum(jnp.sum(centred * centred, axis=1), "col")
     inverse = lax.rsqrt(row_square / full_width + EPSILON)

time: 1180 us -> 1180 us (level)
  waiting for transfers between devices: 650 us -> 637 us
  blocking collectives: 114 us -> 126 us
    unnamed x0 -> x3, blocking collectives: none -> 34.2 us
    psum x3 -> x0, blocking collectives: 25 us -> none  [norm_forward(): row_total = lax.psum(jnp.sum(values, axis=1), 'col')]
  transfers between devices with their start and end apart: 17 -> 17, of which waited for: 16 -> 15; matrix products, arithmetic and copies ran while one was open for 12% -> 12% of each run, Pallas kernels for 0% -> 0%
where the time goes in v1:
time: 1180 us; the launch traced here: 1170 us
  waiting for transfers between devices  637 us (54%)
  matrix products  250 us (21%)
  blocking collectives  126 us (11%)
  other arithmetic  79.1 us (7%)
  local copies, waits for them, and re-layouts  64.6 us (5%)
  between operations  15.5 us (1%)
    reduce_scatter x2, waiting for transfers between devices, sum_grad_partials(): return lax.psum_scatter(values, 'col', scatter_dimension=1, tiled=True)  116 us
    unnamed x19, waiting for transfers between devices  103 us
    reduce_scatter x3, waiting for transfers between devices, sum_partials(): return lax.psum_scatter(values, 'col', scatter_dimension=1, tiled=True)  99.1 us
    reduce_scatter x1, waiting for transfers between devices, per_device(): lax.psum_scatter(expand_grad.astype(jnp.bfloat16), 'row', scatter_dimensi...  68 us
    reduce_scatter x1, waiting for transfers between devices, per_device(): lax.psum_scatter(inward_grad.astype(jnp.bfloat16), 'row', scatter_dimensi...  67.1 us
    all_gather x2, waiting for transfers between devices, spread_grads(): return lax.all_gather(values, 'col', axis=1, tiled=True)  59.7 us
    all_gather x3, waiting for transfers between devices, spread_features(): return lax.all_gather(values, 'col', axis=1, tiled=True)  53.9 us
    all_gather x1, waiting for transfers between devices, fetch_weights(): lax.all_gather(reduce_weight, 'row', axis=1, tiled=True)  44.5 us
  transfers between devices with their start and end apart: 17, of which 15 were waited for; matrix products, arithmetic and copies ran while one was open for 12% of the time, Pallas kernels for 0%

profile of v1, /device:TPU:0, one launch (start us, length us, event | category | flops | bytes accessed | tf_op | source)
XLA Modules:
  0.0 1173.8 jit_solution(4455379884463826610)
XLA Ops:
  11.9 12.8 %all-reduce = f32[6272]{0:T(1024)S(1)} all-reduce(f32[6272]{0:T(1024)S(1)} %dynamic-update-slice), channel_id=2, replica_groups=mesh['row'=8,'col'=4] {'col'}, use_global_device_ids=true, to_apply=%add | all-reduce | flops 6272 | bytes 50176
  34.6 33.1 %all_gather.56 = bf16[256,1024]{1,0:T(8,128)(2,1)} all-gather(bf16[256,128]{1,0:T(8,128)(2,1)S(1)} %copy-done.18), channel_id=1, replica_groups=mesh['row'=8,'col'=4] {'row'}, dimensions={1}, use_global_device_ids=true | all-gather | bytes 589824 | tf_op jit(solution)/shard_map/all_gather | solution.py:52
  69.5 24.1 %all-gather.12.cloned.1.call-done = bf16[1568,1024]{1,0:T(8,128)(2,1)} async-done(((bf16[1568,256]{1,0:T(8,128)(2,1)}), bf16[1568,1024]{1,0:T(8,128)(2,1)}) %all-gather.12.cloned.1.call-update) | async-done | bytes 3211280 | tf_op jit(solution)/shard_map/all_gather | solution.py:34
  110.1 34.0 %while.64 = (s32[]{:T(128)}, bf16[2,784,4,64]{1,3,2,0:T(8,128)(2,1)S(1)}, bf16[2,784,4,64]{1,3,2,0:T(8,128)(2,1)}, bf16[1568,4,64]{0,2,1:T(8,128)(2,1)}, bf16[1568,4,64]{0,2,1:T(8,128)(2,1)}, /*index=5*/s32[]{:T(128)}) while((s32[]{:T(128)}, bf16[2,784,4,64]{1,3,2,0:T(8,128)(2,1)S(1)}, bf16[2,784,4,64]{1,3,2,0:T(8,128)(2,1)}, ...), condition=%wide.region_7.0_spmd, body=%wide.region_4.7_spmd.sunk | while | flops 1922650112 | bytes 4304209 | solution.py:76
  150.5 30.1 %while.65 = (s32[]{:T(128)}, bf16[2,784,4,64]{1,3,2,0:T(8,128)(2,1)}, f32[2,4,784]{2,1,0:T(4,128)S(1)}, bf16[2,784,4,64]{1,3,2,0:T(8,128)(2,1)}, bf16[1568,4,64]...) while((s32[]{:T(128)}, bf16[2,784,4,64]{1,3,2,0:T(8,128)(2,1)}, ...), condition=%wide.region_17.18_spmd, body=%wide.region_14.17_spmd.sunk | while | flops 1303067648 | bytes 62078304 | solution.py:76
  189.1 19.6 %reduce-scatter.14.cloned.1.call-done = f32[1568,256]{1,0:T(8,128)} async-done(((f32[1568,1024]{1,0:T(8,128)}), f32[1568,256]{1,0:T(8,128)}) %reduce-scatter.14.cloned.1.call-update) | async-done | bytes 1605648 | tf_op jit(solution)/shard_map/reduce_scatter | solution.py:38
  208.7 61.9 %reduce-scatter.18.cloned.1.call-done = f32[1568,256]{1,0:T(8,128)} async-done(((f32[1568,1024]{1,0:T(8,128)}), f32[1568,256]{1,0:T(8,128)}) %reduce-scatter.18.cloned.1.call-update) | async-done | bytes 1605648 | tf_op jit(solution)/shard_map/reduce_scatter | solution.py:38
  274.9 10.3 all-reduce.2
  297.0 25.0 %all-gather.18.cloned.1.call-done = bf16[1024,1024]{1,0:T(8,128)(2,1)} async-done(((bf16[128,1024]{1,0:T(8,128)(2,1)}), bf16[1024,1024]{1,0:T(8,128)(2,1)}) %all-gather.18.cloned.1.call-update) | async-done | bytes 2097168 | tf_op jit(solution)/shard_map/all_gather | solution.py:53
  321.9 29.8 %all-gather.22.cloned.1.call-done = bf16[1568,1024]{1,0:T(8,128)(2,1)} async-done(((bf16[1568,256]{1,0:T(8,128)(2,1)}), bf16[1568,1024]{1,0:T(8,128)(2,1)}) %all-gather.22.cloned.1.call-update) | async-done | bytes 3211280 | tf_op jit(solution)/shard_map/all_gather | solution.py:34
  360.4 44.5 %all-gather.20.cloned.1.call-done = bf16[1024,1024]{1,0:T(8,128)(2,1)} async-done(((bf16[1024,128]{1,0:T(8,128)(2,1)}), bf16[1024,1024]{1,0:T(8,128)(2,1)}) %all-gather.20.cloned.1.call-update) | async-done | bytes 2097168 | tf_op jit(solution)/shard_map/all_gather | solution.py:54
  404.9 29.1 %all-gather.24.cloned.1.call-done = bf16[1568,1024]{1,0:T(8,128)(2,1)} async-done(((bf16[1568,256]{1,0:T(8,128)(2,1)}), bf16[1568,1024]{1,0:T(8,128)(2,1)}) %all-gather.24.cloned.1.call-update) | async-done | bytes 3211280 | tf_op jit(solution)/shard_map/all_gather | solution.py:42
  434.0 22.4 %convert_reduce_fusion = (f32[1024]{0:T(1024)}, bf16[1568,1024]{1,0:T(8,128)(2,1)S(1)}, f32[1568,1024]{1,0:T(8,128)}) fusion(f32[1568,1024]{1,0:T(8,128)} %fusion.142, f32[1024]{0:T(1024)S(1)} %copy-done.34, bf16[1568,1024]{1,0:T(8,128)(2,1)} %all-gather.24.cloned.1.call-done, bf16[1024,1024]{1,0:T(8,128)(2,1)} %all-gather.20.cloned.1.call-done), kind=kOutput, calls=%fused_computation.69 | convolution fusion | flops 3408755712 | bytes 21372928 | tf_op jit(solution)/shard_map/dot_general | solution.py:258
  464.1 58.8 %reduce-scatter.20.cloned.1.call-done = f32[1568,256]{1,0:T(8,128)} async-done(((f32[1568,1024]{1,0:T(8,128)}), f32[1568,256]{1,0:T(8,128)}) %reduce-scatter.20.cloned.1.call-update) | async-done | bytes 1605648 | tf_op jit(solution)/shard_map/reduce_scatter | solution.py:46
  525.9 11.1 all-reduce.5
  541.0 30.6 %all-gather.26.cloned.1.call-done = bf16[1568,1024]{1,0:T(8,128)(2,1)} async-done(((bf16[1568,256]{1,0:T(8,128)(2,1)}), bf16[1568,1024]{1,0:T(8,128)(2,1)}) %all-gather.26.cloned.1.call-update) | async-done | bytes 3211280 | tf_op jit(solution)/shard_map/all_gather | solution.py:42
  579.2 129.4 %while.66 = (s32[]{:T(128)}, f32[1568,4,64]{0,2,1:T(8,128)}, f32[1568,4,64]{0,2,1:T(8,128)}, bf16[2,784,4,64]{1,3,2,0:T(8,128)(2,1)}, bf16[2,784,4,64]{1,3,2,0:T...) while((s32[]{:T(128)}, f32[1568,4,64]{0,2,1:T(8,128)}, ...), condition=%wide.region_30.31_spmd.clone, body=%wide.region_28.30_spmd.clone.sunk | while | flops 3188179968 | bytes 291960320 | solution.py:113
  579.2 11.1 fusion.222
  590.4 13.9 %multiply_reduce_fusion.15 = (f32[4,784]{1,0:T(4,128)S(1)}, f32[4,784,1568]{2,1,0:T(8,128)}) fusion(f32[4,784,1568]{2,1,0:T(8,128)} %fusion.222, f32[4,784]{1,0:T(4,128)S(1)} %dynamic-slice_bitcast_fusion.2, bf16[1568,4,64]{0,2,1:T(8,128)(2,1)} %get-tuple-element.583, bf16[2,784,4,64]{1,3,2,0:T(8,128)(2,1)} %get-tuple-element.582, s32[]{:T(128)S(6)} %copy.125), kind=kOutput, calls=%fused_computation.37.clone.1 | convolution fusion | flops 649073600 | bytes 41878020 | tf_op jit(solution)/shard_map/while/body/eval_jaxpr/while/body/eval_jaxpr/qhd,khd->hqk/dot_general | solution.py:88
  604.2 18.2 %multiply_convert_fusion.6 = bf16[4,784,1568]{2,1,0:T(8,128)(2,1)} fusion(f32[4,784,1568]{2,1,0:T(8,128)} %get-tuple-element.515, f32[4,784,1568]{2,1,0:T(8,128)} %fusion.222, f32[4,784]{1,0:T(4,128)S(1)} %get-tuple-element.516), kind=kLoop, calls=%fused_computation.36.clone.1 | loop fusion | flops 14751744 | bytes 49185024 | tf_op jit(solution)/shard_map/while/body/eval_jaxpr/while/body/eval_jaxpr/convert_element_type | solution.py:96
  643.6 11.1 fusion.222
  654.7 13.9 %multiply_reduce_fusion.15 = (f32[4,784]{1,0:T(4,128)S(1)}, f32[4,784,1568]{2,1,0:T(8,128)}) fusion(f32[4,784,1568]{2,1,0:T(8,128)} %fusion.222, f32[4,784]{1,0:T(4,128)S(1)} %dynamic-slice_bitcast_fusion.2, bf16[1568,4,64]{0,2,1:T(8,128)(2,1)} %get-tuple-element.583, bf16[2,784,4,64]{1,3,2,0:T(8,128)(2,1)} %get-tuple-element.582, s32[]{:T(128)S(6)} %copy.125), kind=kOutput, calls=%fused_computation.37.clone.1 | convolution fusion | flops 649073600 | bytes 41878020 | tf_op jit(solution)/shard_map/while/body/eval_jaxpr/while/body/eval_jaxpr/qhd,khd->hqk/dot_general | solution.py:88
  668.6 18.2 %multiply_convert_fusion.6 = bf16[4,784,1568]{2,1,0:T(8,128)(2,1)} fusion(f32[4,784,1568]{2,1,0:T(8,128)} %get-tuple-element.515, f32[4,784,1568]{2,1,0:T(8,128)} %fusion.222, f32[4,784]{1,0:T(4,128)S(1)} %get-tuple-element.516), kind=kLoop, calls=%fused_computation.36.clone.1 | loop fusion | flops 14751744 | bytes 49185024 | tf_op jit(solution)/shard_map/while/body/eval_jaxpr/while/body/eval_jaxpr/convert_element_type | solution.py:96
  727.2 57.5 %reduce-scatter.22.cloned.1.call-done = f32[1568,256]{1,0:T(8,128)} async-done(((f32[1568,1024]{1,0:T(8,128)}), f32[1568,256]{1,0:T(8,128)}) %reduce-scatter.22.cloned.1.call-update) | async-done | bytes 1605648 | tf_op jit(solution)/shard_map/reduce_scatter | solution.py:46
  798.9 11.4 fusion.95
  836.6 23.6 %fusion.94 = f32[1568,1024]{1,0:T(8,128)} fusion(bf16[1024,1024]{1,0:T(8,128)(2,1)} %all-gather.20.cloned.1.call-done, bf16[1568,1024]{1,0:T(8,128)(2,1)} %all-gather.16.cloned.1.call-done, bf16[1024,1024]{1,0:T(8,128)(2,1)} %all-gather.18.cloned.1.call-done, f32[1024]{0:T(1024)S(1)} %copy-done.35), kind=kOutput, calls=%fused_computation.110 | convolution fusion | flops 6682640384 | bytes 13832192 | tf_op jit(solution)/shard_map/dot_general | solution.py:169
  860.2 40.4 %reduce-scatter.30.cloned.1.call-done = bf16[128,1024]{1,0:T(8,128)(2,1)} async-done(((bf16[1024,1024]{1,0:T(8,128)(2,1)}), bf16[128,1024]{1,0:T(8,128)(2,1)}) %reduce-scatter.30.cloned.1.call-update) | async-done | bytes 262160
  902.7 68.0 %reduce-scatter.26.cloned.1.call-done = bf16[128,1024]{1,0:T(8,128)(2,1)} async-done(((bf16[1024,1024]{1,0:T(8,128)(2,1)}), bf16[128,1024]{1,0:T(8,128)(2,1)}) %reduce-scatter.26.cloned.1.call-update) | async-done | bytes 262160 | tf_op jit(solution)/shard_map/reduce_scatter | solution.py:340
  974.1 60.7 %reduce-scatter.28.cloned.1.call-done = bf16[128,256]{1,0:T(8,128)(2,1)} async-done(((bf16[1024,256]{1,0:T(8,128)(2,1)}), bf16[128,256]{1,0:T(8,128)(2,1)}) %reduce-scatter.28.cloned.1.call-update) | async-done | bytes 65552
  1036.4 67.1 %reduce-scatter.24.cloned.1.call-done = bf16[128,3,256]{2,0,1:T(8,128)(2,1)} async-done(((bf16[1024,3,256]{2,0,1:T(8,128)(2,1)}), bf16[128,3,256]{2,0,1:T(8,128)(2,1)}) %reduce-scatter.24.cloned.1.call-update) | async-done | bytes 196624 | tf_op jit(solution)/shard_map/reduce_scatter | solution.py:334
  1111.5 35.2 %all-reduce.3 = (f32[256]{0:T(256)}, f32[256]{0:T(256)}, f32[2,256]{1,0:T(2,128)}, f32[256]{0:T(256)}, f32[256]{0:T(256)}, /*index=5*/f32[256]{0:T(256)}, f32[1024]{0:T(1024)}, f32[256]{0:T(256)}) all-reduce(f32[256]{0:T(256)S(1)} %get-tuple-element.301, f32[256]{0:T(256)S(1)} %get-tuple-element.308, ...), channel_id=1, replica_groups=mesh['row'=8,'col'=4] {'row'}, use_global_device_ids=true, to_apply=%region_37.38 | all-reduce | flops 3072 | bytes 24576 | tf_op jit(solution)/shard_map/psum | solution.py:356
  1146.7 17.6 %reduce-scatter.16.cloned.1.call-done = f32[1568,256]{1,0:T(8,128)} async-done(((f32[1568,1024]{1,0:T(8,128)}), f32[1568,256]{1,0:T(8,128)}) %reduce-scatter.16.cloned.1.call-update) | async-done | bytes 1605648 | tf_op jit(solution)/shard_map/reduce_scatter | solution.py:38
  (231 shorter events, 276.8 us)
Async XLA Ops:
  7.2 60.5 %all-gather.14.cloned.1.call-start = ((), (), s32[]{:S(2)}) async-start(), calls=%async_computation.10 | async-start | bytes 1769472 | tf_op jit(solution)/shard_map/all_gather | solution.py:51
  7.9 85.6 %all-gather.12.cloned.1.call-start = ((), (), s32[]{:S(2)}) async-start(), calls=%async_computation.9 | async-start | bytes 4014080 | tf_op jit(solution)/shard_map/all_gather | solution.py:34
  9.3 88.8 %copy-start.2 = (f32[1568,256]{1,0:T(8,128)}, f32[1568,256]{1,0:T(8,128)S(1)}, u32[]{:S(2)}) copy-start(f32[1568,256]{1,0:T(8,128)S(1)} %reshape.171) | copy-start | bytes 4816900
  34.4 174.4 %reduce-scatter.14.cloned.1.call-start = ((), (), s32[]{:S(2)}) async-start(), calls=%async_computation.11 | async-start | bytes 8028160 | tf_op jit(solution)/shard_map/reduce_scatter | solution.py:38
  149.4 121.3 %reduce-scatter.18.cloned.1.call-start = ((), (), s32[]{:S(2)}) async-start(), calls=%async_computation.16 | async-start | bytes 8028160 | tf_op jit(solution)/shard_map/reduce_scatter | solution.py:38
  183.3 87.3 %copy-start.3 = (f32[1568,256]{1,0:T(8,128)S(1)}, f32[1568,256]{1,0:T(8,128)}, u32[]{:S(2)}) copy-start(f32[1568,256]{1,0:T(8,128)} %copy-done.2) | copy-start | bytes 4816900
  183.3 87.3 %copy-start.31 = (f32[256]{0:T(256)S(1)}, f32[256]{0:T(256)}, u32[]{:S(2)}) copy-start(f32[256]{0:T(256)} %param.26) | copy-start | bytes 3076
  188.5 104.1 %copy-start.20 = (f32[256]{0:T(256)S(1)}, f32[256]{0:T(256)}, u32[]{:S(2)}) copy-start(f32[256]{0:T(256)} %param.27) | copy-start | bytes 3076
  188.5 104.1 %copy-start.23 = (f32[256]{0:T(256)S(1)}, f32[256]{0:T(256)}, u32[]{:S(2)}) copy-start(f32[256]{0:T(256)} %param.28) | copy-start | bytes 3076
  188.5 133.4 %all-gather.18.cloned.1.call-start = ((), (), s32[]{:S(2)}) async-start(), calls=%async_computation.13 | async-start | bytes 2359296 | tf_op jit(solution)/shard_map/all_gather | solution.py:53
  189.1 162.6 %all-gather.22.cloned.1.call-start = ((), (), s32[]{:S(2)}) async-start(), calls=%async_computation.17 | async-start | bytes 4014080 | tf_op jit(solution)/shard_map/all_gather | solution.py:34
  294.0 110.9 %all-gather.20.cloned.1.call-start = ((), (), s32[]{:S(2)}) async-start(), calls=%async_computation.14 | async-start | bytes 2359296 | tf_op jit(solution)/shard_map/all_gather | solution.py:54
  294.7 139.2 %all-gather.24.cloned.1.call-start = ((), (), s32[]{:S(2)}) async-start(), calls=%async_computation.18 | async-start | bytes 4014080 | tf_op jit(solution)/shard_map/all_gather | solution.py:42
  296.9 137.1 %copy-start.34 = (f32[1024]{0:T(1024)S(1)}, f32[1024]{0:T(1024)}, u32[]{:S(2)}) copy-start(f32[1024]{0:T(1024)} %param.30) | copy-start | bytes 12292
  296.9 226.0 %reduce-scatter.20.cloned.1.call-start = ((), (), s32[]{:S(2)}) async-start(), calls=%async_computation.19 | async-start | bytes 8028160 | tf_op jit(solution)/shard_map/reduce_scatter | solution.py:46
  463.5 73.5 %copy-start.9 = (bf16[1568,256]{1,0:T(8,128)(2,1)S(1)}, bf16[1568,256]{1,0:T(8,128)(2,1)}, u32[]{:S(2)}) copy-start(bf16[1568,256]{1,0:T(8,128)(2,1)} %reshape.168) | copy-start | bytes 2408452
  463.6 108.0 %copy-start.13 = (bf16[256,1024]{1,0:T(8,128)(2,1)S(1)}, bf16[256,1024]{1,0:T(8,128)(2,1)}, u32[]{:S(2)}) copy-start(bf16[256,1024]{1,0:T(8,128)(2,1)} %all_gather.56) | copy-start | bytes 1572868
  463.6 108.0 %all-gather.26.cloned.1.call-start = ((), (), s32[]{:S(2)}) async-start(), calls=%async_computation.20 | async-start | bytes 4014080 | tf_op jit(solution)/shard_map/all_gather | solution.py:42
  540.9 243.8 %reduce-scatter.22.cloned.1.call-start = ((), (), s32[]{:S(2)}) async-start(), calls=%async_computation.21 | async-start | bytes 8028160 | tf_op jit(solution)/shard_map/reduce_scatter | solution.py:46
  725.3 73.6 %copy-start.35 = (f32[1024]{0:T(1024)S(1)}, f32[1024]{0:T(1024)}, u32[]{:S(2)}) copy-start(f32[1024]{0:T(1024)} %param.30) | copy-start | bytes 12292
  725.4 111.2 %all-gather.16.cloned.1.call-start = ((), (), s32[]{:S(2)}) async-start(), calls=%async_computation.12 | async-start | bytes 4014080 | tf_op jit(solution)/shard_map/all_gather | solution.py:34
  798.8 101.8 %reduce-scatter.30.cloned.1.call-start = ((), (), s32[]{:S(2)}) async-start(), calls=%async_computation.25 | async-start | bytes 2359296
  814.3 156.3 %reduce-scatter.26.cloned.1.call-start = ((), (), s32[]{:S(2)}) async-start(), calls=%async_computation.23 | async-start | bytes 2359296 | tf_op jit(solution)/shard_map/reduce_scatter | solution.py:340
  823.1 211.7 %reduce-scatter.28.cloned.1.call-start = ((), (), s32[]{:S(2)}) async-start(), calls=%async_computation.24 | async-start | bytes 589824
  829.4 274.2 %reduce-scatter.24.cloned.1.call-start = ((), (), s32[]{:S(2)}) async-start(), calls=%async_computation.22 | async-start | bytes 1769472 | tf_op jit(solution)/shard_map/reduce_scatter | solution.py:334
  836.3 327.9 %reduce-scatter.16.cloned.1.call-start = ((), (), s32[]{:S(2)}) async-start(), calls=%async_computation.15 | async-start | bytes 8028160 | tf_op jit(solution)/shard_map/reduce_scatter | solution.py:38
  902.6 208.8 %copy-start.25 = (f32[256]{0:T(256)S(1)}, f32[256]{0:T(256)}, u32[]{:S(2)}) copy-start(f32[256]{0:T(256)} %get-tuple-element.299) | copy-start | bytes 3076
  902.6 208.8 %copy-start.26 = (f32[256]{0:T(256)S(1)}, f32[256]{0:T(256)}, u32[]{:S(2)}) copy-start(f32[256]{0:T(256)} %get-tuple-element.307) | copy-start | bytes 3076
  902.6 208.8 %copy-start.27 = (f32[256]{0:T(256)S(1)}, f32[256]{0:T(256)}, u32[]{:S(2)}) copy-start(f32[256]{0:T(256)} %get-tuple-element.368) | copy-start | bytes 3076
  902.6 208.8 %copy-start.28 = (f32[256]{0:T(256)S(1)}, f32[256]{0:T(256)}, u32[]{:S(2)}) copy-start(f32[256]{0:T(256)} %get-tuple-element.383) | copy-start | bytes 3076
  902.6 208.8 %copy-start.29 = (f32[1024]{0:T(1024)S(1)}, f32[1024]{0:T(1024)}, u32[]{:S(2)}) copy-start(f32[1024]{0:T(1024)} %get-tuple-element.365) | copy-start | bytes 12292
  902.6 261.6 %copy-start.32 = (f32[256]{0:T(256)S(1)}, f32[256]{0:T(256)}, u32[]{:S(2)}) copy-start(f32[256]{0:T(256)} %param.32) | copy-start | bytes 3076
  (26 other events, 638.4 us)
Sparse Core Ops, SparseCore 0:
  10.2 50.4 all-gather.13
  62.9 30.5 all-gather.11
  149.5 59.2 reduce-scatter.13
  211.3 59.2 reduce-scatter.17
  272.6 49.2 all-gather.17
  323.9 27.7 all-gather.21
  353.8 51.0 all-gather.19
  406.4 27.4 all-gather.23
  463.7 59.2 reduce-scatter.19
  541.0 30.4 all-gather.25
  725.5 59.2 reduce-scatter.21
  798.9 30.3 all-gather.15
  832.9 67.7 reduce-scatter.29
  904.1 66.5 reduce-scatter.25
  973.8 60.9 reduce-scatter.27
  1039.1 64.4 reduce-scatter.23
  1106.0 58.2 reduce-scatter.15
